TPU v7x, 32 devices: a whole 2x2x4 slice. The times are simulated.
32 devices in a mesh: dp: 4 (over z), ctx: 8 (over y, x, core).
Axes of the slice: x: 2, y: 2, z: 4, core: 2. Of those that a mesh axis runs over, the one named last changes fastest.
Arguments:
- queries: bfloat16 [4, 4096, 1024], P('dp', 'ctx'), may hold values from -6 to 6
- key_vectors: bfloat16 [4, 4096, 1024], P('dp', 'ctx'), may hold values from -6 to 6
- value_vectors: bfloat16 [4, 4096, 1024], P('dp', 'ctx'), may hold values from -6 to 6
- out_grad: bfloat16 [4, 4096, 1024], P('dp', 'ctx'), may hold values from -6 to 6
- column_bias: float32 [8], replicated, may hold values from -1 to 2
- column_offsets: int32 [1], replicated, may hold values from 0 to 63
Outputs:
- attended: bfloat16 [4, 4096, 1024], P('dp', 'ctx')
- query_grad: bfloat16 [4, 4096, 1024], P('dp', 'ctx')
- key_grad: bfloat16 [4, 4096, 1024], P('dp', 'ctx')
- value_grad: bfloat16 [4, 4096, 1024], P('dp', 'ctx')
- bias_grad: float32 [8], replicated
All inputs are finite; a program needn't handle non-finite values.
Results may differ from a plain program's by a relative error of at most 0.005.
The roundings to bfloat16 on the way count: a program that leaves them out, or rounds other values in their place, can miss the bound.
Values may be sent and summed in bfloat16 or wider, within the bound.
A program may use at most 128 MiB of HBM per device.

v0:
```python
import jax
import jax.numpy as jnp
from jax import lax
from jax.sharding import PartitionSpec as P

HEADS = 8
HEAD_DIM = 128
LOCAL_BAND = 512
STRIDE = 4096
CB = 64
TOKENS_PER_SHARD = 512


def from_behind(value, axis, by):
    size = lax.axis_size(axis)
    pairs = [(i, i + by) for i in range(size) if 0 <= i + by < size]
    return lax.ppermute(value, axis, pairs)


def column_flags(positions, offsets):
    window = positions // STRIDE
    within = positions % STRIDE
    picks = window[:, None] == jnp.arange(offsets.shape[0], dtype=jnp.int32)[None, :]
    offset_at = jnp.sum(jnp.where(picks, offsets[None, :], 0), axis=1)
    return (positions >= 0) & (within // CB == offset_at)


def head_block(qh, kb, vb, kc, vc, doh, bias_h, band_ok, band_col, col_ok):
    scale = HEAD_DIM ** (-0.5)
    sb = (
        jnp.dot(qh, kb.T, preferred_element_type=jnp.float32) * scale
        + jnp.where(band_col, bias_h, 0.0)[None, :]
    )
    sc = jnp.dot(qh, kc.T, preferred_element_type=jnp.float32) * scale + bias_h
    sb = jnp.where(band_ok, sb, -jnp.inf)
    sc = jnp.where(col_ok, sc, -jnp.inf)
    top = jnp.maximum(jnp.max(sb, axis=1), jnp.max(sc, axis=1))
    pb = jnp.exp(sb - top[:, None])
    pc = jnp.exp(sc - top[:, None])
    total = jnp.sum(pb, axis=1) + jnp.sum(pc, axis=1)
    wb = pb / total[:, None]
    wc = pc / total[:, None]
    wb16 = wb.astype(jnp.bfloat16)
    wc16 = wc.astype(jnp.bfloat16)
    mixed = jnp.dot(wb16, vb, preferred_element_type=jnp.float32) + jnp.dot(
        wc16, vc, preferred_element_type=jnp.float32
    )
    oh = mixed.astype(jnp.bfloat16)
    delta = jnp.sum(doh.astype(jnp.float32) * oh.astype(jnp.float32), axis=1)
    dsb = wb * (jnp.dot(doh, vb.T, preferred_element_type=jnp.float32) - delta[:, None])
    dsc = wc * (jnp.dot(doh, vc.T, preferred_element_type=jnp.float32) - delta[:, None])
    dbias = jnp.sum(jnp.where(band_col[None, :], dsb, 0.0)) + jnp.sum(dsc)
    dsb16 = dsb.astype(jnp.bfloat16)
    dsc16 = dsc.astype(jnp.bfloat16)
    dq = (
        (
            jnp.dot(dsb16, kb, preferred_element_type=jnp.float32)
            + jnp.dot(dsc16, kc, preferred_element_type=jnp.float32)
        )
        * scale
    ).astype(jnp.bfloat16)
    dkb = jnp.dot(dsb16.T, qh, preferred_element_type=jnp.float32) * scale
    dvb = jnp.dot(wb16.T, doh, preferred_element_type=jnp.float32)
    dkc = jnp.dot(dsc16.T, qh, preferred_element_type=jnp.float32) * scale
    dvc = jnp.dot(wc16.T, doh, preferred_element_type=jnp.float32)
    return (oh, dq, dkb, dvb, dkc, dvc, dbias, top, total, delta)


def separate_heads(x):
    return x.reshape(x.shape[0], HEADS, HEAD_DIM).transpose(1, 0, 2)


def join_heads(x):
    return x.transpose(1, 0, 2).reshape(x.shape[1], HEADS * HEAD_DIM)


def per_device(queries, key_vectors, value_vectors, out_grad, column_bias, column_offsets):
    here = lax.axis_index("ctx")
    count = lax.axis_size("ctx")
    start_position = here * TOKENS_PER_SHARD
    width = queries.shape[2]
    query_rows = queries[0]
    key_rows = key_vectors[0]
    value_rows = value_vectors[0]
    grad_rows = out_grad[0]
    ncol = column_offsets.shape[0]
    block_starts = jnp.arange(ncol, dtype=jnp.int32) * STRIDE + column_offsets * CB
    colpos = jnp.repeat(block_starts, CB) + jnp.tile(jnp.arange(CB, dtype=jnp.int32), ncol)
    window = start_position // STRIDE
    own_start = window * STRIDE + column_offsets[window] * CB
    local = jnp.clip(own_start - start_position, 0, TOKENS_PER_SHARD - CB)
    piece_k = lax.dynamic_slice_in_dim(key_rows, local, CB, 0)
    piece_v = lax.dynamic_slice_in_dim(value_rows, local, CB, 0)
    pieces_k, pieces_v = (
        lax.all_gather(piece_k, "ctx", axis=0, tiled=True),
        lax.all_gather(piece_v, "ctx", axis=0, tiled=True),
    )
    owner = block_starts // TOKENS_PER_SHARD
    col_k = pieces_k.reshape(count, CB, width)[owner].reshape(ncol * CB, width)
    col_v = pieces_v.reshape(count, CB, width)[owner].reshape(ncol * CB, width)
    prev_k, prev_v = from_behind((key_rows, value_rows), "ctx", 1)
    band_k = jnp.concatenate([prev_k, key_rows], axis=0)
    band_v = jnp.concatenate([prev_v, value_rows], axis=0)
    qpos = start_position + jnp.arange(TOKENS_PER_SHARD, dtype=jnp.int32)
    kpos = start_position - LOCAL_BAND + jnp.arange(LOCAL_BAND + TOKENS_PER_SHARD, dtype=jnp.int32)
    gap = qpos[:, None] - kpos[None, :]
    band_ok = (kpos[None, :] >= 0) & (gap >= 0) & (gap < LOCAL_BAND)
    band_col = column_flags(kpos, column_offsets)
    col_ok = colpos[None, :] <= qpos[:, None] - LOCAL_BAND

    def per_head(items):
        return head_block(
            items[0],
            items[1],
            items[2],
            items[3],
            items[4],
            items[5],
            items[6],
            band_ok,
            band_col,
            col_ok,
        )

    results = lax.map(
        per_head,
        (
            separate_heads(query_rows),
            separate_heads(band_k),
            separate_heads(band_v),
            separate_heads(col_k),
            separate_heads(col_v),
            separate_heads(grad_rows),
            column_bias,
        ),
    )
    oh, dq, dkb, dvb, dkc, dvc, dbias, top, total, delta = results
    attended = join_heads(oh)
    query_grad = join_heads(dq)
    dk_band = join_heads(dkb)
    dv_band = join_heads(dvb)
    own_dk = dk_band[dk_band.shape[0] - TOKENS_PER_SHARD :]
    own_dv = dv_band[dv_band.shape[0] - TOKENS_PER_SHARD :]
    back_k, back_v = from_behind((dk_band[:LOCAL_BAND], dv_band[:LOCAL_BAND]), "ctx", -1)
    own_dk = own_dk.at[TOKENS_PER_SHARD - LOCAL_BAND :].add(back_k)
    own_dv = own_dv.at[TOKENS_PER_SHARD - LOCAL_BAND :].add(back_v)
    summed_k, summed_v = lax.psum((join_heads(dkc), join_heads(dvc)), "ctx")
    flags = column_flags(qpos, column_offsets)
    source = jnp.clip(qpos // STRIDE * CB + qpos % CB, 0, ncol * CB - 1)
    own_dk = own_dk + jnp.where(flags[:, None], summed_k[source], 0.0)
    own_dv = own_dv + jnp.where(flags[:, None], summed_v[source], 0.0)
    bias_grad = lax.psum(dbias, ("dp", "ctx"))
    return (
        attended[None],
        query_grad[None],
        own_dk.astype(jnp.bfloat16)[None],
        own_dv.astype(jnp.bfloat16)[None],
        bias_grad,
    )


def solution(mesh):
    placed = (
        P("dp", "ctx", None),
        P("dp", "ctx", None),
        P("dp", "ctx", None),
        P("dp", "ctx", None),
        P(),
        P(),
    )
    return jax.shard_map(
        per_device,
        mesh=mesh,
        in_specs=placed,
        out_specs=(
            P("dp", "ctx", None),
            P("dp", "ctx", None),
            P("dp", "ctx", None),
            P("dp", "ctx", None),
            P(),
        ),
        check_vma=False,
    )
```

profile of v0, /device:TPU:0, one launch (start us, length us, event | category | flops | bytes accessed | tf_op | source)
XLA Modules:
  0.0 354.4 jit_solution(14615889557479074196)
XLA Ops:
  12.8 3.3 collective-permute-start
  16.7 4.5 %collective-permute-start.1 = (bf16[512,1024]{0,1:T(8,128)(2,1)S(1)}, bf16[512,1024]{0,1:T(8,128)(2,1)}, u32[]{:S(2)}, u32[]{:S(2)}) collective-permute-start(bf16[512,1024]{0,1:T(8,128)(2,1)S(1)} %bitcast.242), channel_id=1, source_target_pairs={{0,1},{1,2},{2,3},{3,4},{4,5},{5,6},{6,7},{8,9},{9,10},{10,11},{11... | collective-permute-start | bytes 3145736 | tf_op jit(solution)/shard_map/ppermute | solution.py:17
  22.7 2.3 copy.26
  25.1 2.9 maximum_bitcast_fusion
  28.0 2.9 maximum_bitcast_fusion.1
  30.9 7.3 %all-gather.7.cloned.1.call-done = bf16[1,512,1024]{2,1,0:T(8,128)(2,1)} async-done(((bf16[1,64,1024]{2,1,0:T(8,128)(2,1)}), bf16[1,512,1024]{2,1,0:T(8,128)(2,1)}) %all-gather.7.cloned.1.call-update) | async-done | bytes 1048592 | tf_op jit(solution)/shard_map/all_gather | solution.py:96
  38.2 25.5 %all-gather.5.cloned.1.call-done = bf16[1,512,1024]{2,1,0:T(8,128)(2,1)} async-done(((bf16[1,64,1024]{2,1,0:T(8,128)(2,1)}), bf16[1,512,1024]{2,1,0:T(8,128)(2,1)}) %all-gather.5.cloned.1.call-update) | async-done | bytes 1048592 | tf_op jit(solution)/shard_map/all_gather | solution.py:95
  65.4 169.8 %while.29 = (s32[]{:T(128)}, bf16[8,512,128]{1,2,0:T(8,128)(2,1)}, bf16[8,512,128]{2,1,0:T(8,128)(2,1)}, f32[8,1024,128]{2,1,0:T(8,128)}, f32[8,1024,128]{2,1,0:...) while((s32[]{:T(128)}, bf16[8,512,128]{1,2,0:T(8,128)(2,1)}, ...), condition=%wide.region_8.9_spmd.clone, body=%wide.region_0.8_spmd.clone.sunk | while | flops 869654016 | bytes 19551504 | solution.py:125
  77.8 2.5 select_reduce_fusion.2
  99.0 2.5 select_reduce_fusion.2
  109.8 2.0 fusion.160
  120.2 2.5 select_reduce_fusion.2
  141.4 2.5 select_reduce_fusion.2
  162.7 2.5 select_reduce_fusion.2
  183.9 2.5 select_reduce_fusion.2
  205.1 2.5 select_reduce_fusion.2
  215.9 2.0 fusion.160
  226.4 2.5 select_reduce_fusion.2
  235.3 4.0 %slice_bitcast_fusion.3 = (f32[8,64,8,128]{3,2,1,0:T(8,128)}, f32[8,64,8,128]{3,2,1,0:T(8,128)S(1)}) fusion(f32[1024,8,128]{2,0,1:T(8,128)} %bitcast.240), kind=kLoop, calls=%fused_computation.130 | loop fusion | bytes 8388608
  248.4 79.4 %psum.23 = f32[8]{0:T(128)} all-reduce(f32[8]{0:T(128)S(1)} %get-tuple-element.149), channel_id=1, replica_groups=mesh['dp'=4,'ctx'=8] {'dp','ctx'}, use_global_device_ids=true, to_apply=%region_11.12 | all-reduce | flops 8 | bytes 64 | tf_op jit(solution)/shard_map/psum | solution.py:152
  331.1 4.3 %all-reduce.3.cloned.1.call-done = (f32[64,1024]{1,0:T(8,128)}, f32[64,1024]{1,0:T(8,128)}) async-done(((f32[64,1024]{1,0:T(8,128)}, f32[64,1024]{1,0:T(8,128)}), (f32[64,1024]{1,0:T(8,128)}, f32[64,1024]{1,0:T(8,128)})) %all-reduce.3.cloned.1.call-update) | async-done | bytes 524304 | tf_op jit(solution)/shard_map/psum | solution.py:147
  335.3 3.8 %gather_fusion = f32[512,1024]{1,0:T(8,128)S(1)} fusion(f32[64,1024]{1,0:T(8,128)} %get-tuple-element.315, s32[1024]{0:T(1024)S(1)} %pad_clamp_fusion), kind=kCustom, calls=%fused_computation | custom fusion | bytes 4196352 | tf_op jit(solution)/shard_map/gather | solution.py:150
  339.2 2.7 gather_fusion.1
  341.8 6.0 %fusion.99 = (bf16[1,512,1024]{2,1,0:T(8,128)(2,1)}, bf16[1,512,1024]{2,1,0:T(8,128)(2,1)}) fusion(f32[512,1024]{1,0:T(8,128)} %gather_fusion.1, f32[512,1024]{1,0:T(8,128)} %collective-permute-done.3, f32[8,64,8,128]{3,2,1,0:T(8,128)} %get-tuple-element.327, pred[512]{0:T(512)(128)(4,1)S(1)} %fusion.108, f32[512,1024]{1,0:T(8,128)S(1)} %gather_fusion, ...), kind=kLoop, calls=%fused_computation.134 | loop fusion | flops 4194304 | bytes 14680576 | tf_op jit(solution)/shard_map/convert_element_type | solution.py:157
  (220 shorter events, 157.1 us)
Async XLA Ops:
  7.2 9.0 %copy-start.3 = (bf16[1,512,1024]{2,1,0:T(8,128)(2,1)S(1)}, bf16[1,512,1024]{2,1,0:T(8,128)(2,1)}, u32[]{:S(2)}) copy-start(bf16[1,512,1024]{2,1,0:T(8,128)(2,1)} %param.18) | copy-start | bytes 3145732
  7.2 31.1 %all-gather.7.cloned.1.call-start = ((), (), s32[]{:S(2)}) async-start(), calls=%async_computation.1 | async-start | bytes 1179648 | tf_op jit(solution)/shard_map/all_gather | solution.py:96
  9.6 54.1 %all-gather.5.cloned.1.call-start = ((), (), s32[]{:S(2)}) async-start(), calls=%async_computation | async-start | bytes 1179648 | tf_op jit(solution)/shard_map/all_gather | solution.py:95
  11.2 324.1 %all-reduce.3.cloned.1.call-start = ((), (), s32[]{:S(2)}) async-start(), calls=%async_computation.2 | async-start | bytes 1048576 | tf_op jit(solution)/shard_map/psum | solution.py:147
  12.8 12.3 %collective-permute-start = (bf16[512,1024]{0,1:T(8,128)(2,1)S(1)}, bf16[512,1024]{0,1:T(8,128)(2,1)}, u32[]{:S(2)}, u32[]{:S(2)}) collective-permute-start(bf16[512,1024]{0,1:T(8,128)(2,1)S(1)} %bitcast.244), channel_id=1, source_target_pairs={{0,1},{1,2},{2,3},{3,4},{4,5},{5,6},{6,7},{8,9},{9,10},{10,11},{11... | collective-permute-start | bytes 3145736 | tf_op jit(solution)/shard_map/ppermute | solution.py:17
  16.7 11.3 %collective-permute-start.1 = (bf16[512,1024]{0,1:T(8,128)(2,1)S(1)}, bf16[512,1024]{0,1:T(8,128)(2,1)}, u32[]{:S(2)}, u32[]{:S(2)}) collective-permute-start(bf16[512,1024]{0,1:T(8,128)(2,1)S(1)} %bitcast.242), channel_id=1, source_target_pairs={{0,1},{1,2},{2,3},{3,4},{4,5},{5,6},{6,7},{8,9},{9,10},{10,11},{11... | collective-permute-start | bytes 3145736 | tf_op jit(solution)/shard_map/ppermute | solution.py:17
  28.0 37.5 %copy-start.2 = (bf16[1,512,1024]{1,2,0:T(8,128)(2,1)S(1)}, bf16[1,512,1024]{1,2,0:T(8,128)(2,1)}, u32[]{:S(2)}) copy-start(bf16[1,512,1024]{1,2,0:T(8,128)(2,1)} %copy.26) | copy-start | bytes 3145732
  28.0 37.5 %copy-start.8 = (f32[8]{0:T(128)S(1)}, f32[8]{0:T(128)}, u32[]{:S(2)}) copy-start(f32[8]{0:T(128)} %param.20) | copy-start | bytes 100
  239.2 3.0 copy-start.1
  240.8 101.0 %collective-permute-start.2 = (f32[512,1024]{1,0:T(8,128)}, f32[512,1024]{1,0:T(8,128)}, u32[]{:S(2)}, u32[]{:S(2)}) collective-permute-start(f32[512,1024]{1,0:T(8,128)} %bitcast.178), channel_id=1, source_target_pairs={{1,0},{2,1},{3,2},{4,3},{5,4},{6,5},{7,6},{9,8},{10,9},{11,10},{12... | collective-permute-start | bytes 6291464 | tf_op jit(solution)/shard_map/ppermute | solution.py:17
  243.9 2.9 copy-start.7
  243.9 3.7 %copy-start.6 = (f32[8,64,128]{2,1,0:T(8,128)S(1)}, f32[8,64,128]{2,1,0:T(8,128)}, u32[]{:S(2)}) copy-start(f32[8,64,128]{2,1,0:T(8,128)} %get-tuple-element.146) | copy-start | bytes 786436
  243.9 83.9 %copy-start.5 = (bf16[8,512,128]{2,1,0:T(8,128)(2,1)S(1)}, bf16[8,512,128]{2,1,0:T(8,128)(2,1)}, u32[]{:S(2)}) copy-start(bf16[8,512,128]{2,1,0:T(8,128)(2,1)} %get-tuple-element.144) | copy-start | bytes 3145732
  245.5 96.3 %collective-permute-start.3 = (f32[512,1024]{1,0:T(8,128)}, f32[512,1024]{1,0:T(8,128)}, u32[]{:S(2)}, u32[]{:S(2)}) collective-permute-start(f32[512,1024]{1,0:T(8,128)} %bitcast.177), channel_id=1, source_target_pairs={{1,0},{2,1},{3,2},{4,3},{5,4},{6,5},{7,6},{9,8},{10,9},{11,10},{12... | collective-permute-start | bytes 6291464 | tf_op jit(solution)/shard_map/ppermute | solution.py:17
  327.8 2.0 copy-start.4
  335.3 3.8 %copy-start = (f32[64,1024]{1,0:T(8,128)S(1)}, f32[64,1024]{1,0:T(8,128)}, u32[]{:S(2)}) copy-start(f32[64,1024]{1,0:T(8,128)} %get-tuple-element.316) | copy-start | bytes 786436
Sparse Core Ops, SparseCore 0:
  9.9 28.2 all-gather.6
  40.1 23.5 all-gather.4
  248.4 86.8 all-reduce.2
where the time goes:
time: 357 us; the launch traced here: 354 us
  matrix products  133 us (37%)
  blocking collectives  79.4 us (22%)
  waiting for transfers between devices  37.1 us (10%)
  local copies, waits for them, and re-layouts  36.4 us (10%)
  other arithmetic  32.7 us (9%)
  between operations  14.7 us (4%)
  starting transfers between devices  10.7 us (3%)
  loops' own time  10 us (3%)
    psum x1, blocking collectives, per_device(): bias_grad = lax.psum(dbias, ('dp', 'ctx'))  79.4 us
    all_gather x1, waiting for transfers between devices, per_device(): lax.all_gather(piece_k, 'ctx', axis=0, tiled=True)  25.5 us
    dot_general x8, matrix products, head_block(): jnp.dot(doh, vb.T, preferred_element_type=jnp.float32) - delta[:, None]  19.7 us
    dot_general x8, matrix products, head_block(): jnp.dot(qh, kb.T, preferred_element_type=jnp.float32) * scale  15.9 us
    unnamed x29, local copies, waits for them, and re-layouts  13.2 us
    dot_general x8, matrix products, head_block(): jnp.dot(wb16, vb, preferred_element_type=jnp.float32)  12.9 us
    dot_general x8, matrix products, head_block(): jnp.dot(wc16, vc, preferred_element_type=jnp.float32)  12.9 us
    dot_general x8, matrix products, head_block(): dvb = jnp.dot(wb16.T, doh, preferred_element_type=jnp.float32)  12.7 us
  transfers between devices with their start and end apart: 7, of which 3 were waited for; matrix products, arithmetic and copies ran while one was open for 8% of the time, Pallas kernels for 0%

commit v1 on v0

--- a/solution.py
+++ b/solution.py
@@ -149,7 +149,9 @@
     source = jnp.clip(qpos // STRIDE * CB + qpos % CB, 0, ncol * CB - 1)
     own_dk = own_dk + jnp.where(flags[:, None], summed_k[source], 0.0)
     own_dv = own_dv + jnp.where(flags[:, None], summed_v[source], 0.0)
-    bias_grad = lax.psum(dbias, ("dp", "ctx"))
+    bias_grad = dbias
+    for k in ("ctx", "dp"):
+        bias_grad = jax.lax.psum(bias_grad, k)
     return (
         attended[None],
         query_grad[None],

time: 357 us -> 341 us (0.955)
  blocking collectives: 79.4 us -> 64.9 us
  waiting for transfers between devices: 37.1 us -> 32.9 us
    psum x1 -> x2, blocking collectives: 79.4 us -> 64.9 us  [per_device(): bias_grad = jax.lax.psum(bias_grad, k)]
    psum x1, waiting for transfers between devices: 4.26 us -> 0.01 us  [per_device(): summed_k, summed_v = lax.psum((join_heads(dkc), join_heads(dvc)), 'ctx')]
  transfers between devices with their start and end apart: 7 -> 7, of which waited for: 3 -> 2; matrix products, arithmetic and copies ran while one was open for 8% -> 8% of each run, Pallas kernels for 0% -> 0%
where the time goes in v1:
time: 341 us; the launch traced here: 337 us
  matrix products  134 us (39%)
  blocking collectives  64.9 us (19%)
  local copies, waits for them, and re-layouts  36.3 us (11%)
  waiting for transfers between devices  32.9 us (10%)
  other arithmetic  32.6 us (10%)
  between operations  14.7 us (4%)
  loops' own time  11 us (3%)
  starting transfers between devices  10.7 us (3%)
    psum x2, blocking collectives, per_device(): bias_grad = jax.lax.psum(bias_grad, k)  64.9 us
    all_gather x1, waiting for transfers between devices, per_device(): lax.all_gather(piece_k, 'ctx', axis=0, tiled=True)  25.5 us
    dot_general x8, matrix products, head_block(): jnp.dot(doh, vb.T, preferred_element_type=jnp.float32) - delta[:, None]  19.7 us
    dot_general x8, matrix products, head_block(): jnp.dot(qh, kb.T, preferred_element_type=jnp.float32) * scale  15.9 us
    unnamed x29, local copies, waits for them, and re-layouts  13.1 us
    dot_general x8, matrix products, head_block(): jnp.dot(wb16, vb, preferred_element_type=jnp.float32)  12.9 us
    dot_general x8, matrix products, head_block(): jnp.dot(wc16, vc, preferred_element_type=jnp.float32)  12.9 us
    dot_general x8, matrix products, head_block(): dvb = jnp.dot(wb16.T, doh, preferred_element_type=jnp.float32)  12.7 us
  transfers between devices with their start and end apart: 7, of which 2 were waited for; matrix products, arithmetic and copies ran while one was open for 8% of the time, Pallas kernels for 0%

profile of v1, /device:TPU:0, one launch (start us, length us, event | category | flops | bytes accessed | tf_op | source)
XLA Modules:
  0.0 337.1 jit_solution(578573277636798815)
XLA Ops:
  12.8 3.3 collective-permute-start
  16.7 4.6 %collective-permute-start.1 = (bf16[512,1024]{0,1:T(8,128)(2,1)S(1)}, bf16[512,1024]{0,1:T(8,128)(2,1)}, u32[]{:S(2)}, u32[]{:S(2)}) collective-permute-start(bf16[512,1024]{0,1:T(8,128)(2,1)S(1)} %bitcast.242), channel_id=1, source_target_pairs={{0,1},{1,2},{2,3},{3,4},{4,5},{5,6},{6,7},{8,9},{9,10},{10,11},{11... | collective-permute-start | bytes 3145736 | tf_op jit(solution)/shard_map/ppermute | solution.py:17
  22.7 2.3 copy.26
  25.1 2.9 maximum_bitcast_fusion
  28.0 2.9 maximum_bitcast_fusion.1
  30.9 7.4 %all-gather.7.cloned.1.call-done = bf16[1,512,1024]{2,1,0:T(8,128)(2,1)} async-done(((bf16[1,64,1024]{2,1,0:T(8,128)(2,1)}), bf16[1,512,1024]{2,1,0:T(8,128)(2,1)}) %all-gather.7.cloned.1.call-update) | async-done | bytes 1048592 | tf_op jit(solution)/shard_map/all_gather | solution.py:96
  38.2 25.5 %all-gather.5.cloned.1.call-done = bf16[1,512,1024]{2,1,0:T(8,128)(2,1)} async-done(((bf16[1,64,1024]{2,1,0:T(8,128)(2,1)}), bf16[1,512,1024]{2,1,0:T(8,128)(2,1)}) %all-gather.5.cloned.1.call-update) | async-done | bytes 1048592 | tf_op jit(solution)/shard_map/all_gather | solution.py:95
  65.4 171.3 %while.29 = (s32[]{:T(128)}, bf16[8,512,128]{1,2,0:T(8,128)(2,1)}, bf16[8,512,128]{2,1,0:T(8,128)(2,1)}, f32[8,1024,128]{2,1,0:T(8,128)}, f32[8,1024,128]{2,1,0:...) while((s32[]{:T(128)}, bf16[8,512,128]{1,2,0:T(8,128)(2,1)}, ...), condition=%wide.region_8.9_spmd.clone, body=%wide.region_0.8_spmd.clone.sunk | while | flops 869654016 | bytes 19551504 | solution.py:125
  67.3 2.0 fusion.160
  77.8 2.5 select_reduce_fusion.2
  99.3 2.5 select_reduce_fusion.2
  120.7 2.5 select_reduce_fusion.2
  142.1 2.5 select_reduce_fusion.2
  153.0 2.0 fusion.160
  163.5 2.5 select_reduce_fusion.2
  184.9 2.5 select_reduce_fusion.2
  206.3 2.5 select_reduce_fusion.2
  227.8 2.5 select_reduce_fusion.2
  236.8 4.0 %slice_bitcast_fusion.3 = (f32[8,64,8,128]{3,2,1,0:T(8,128)}, f32[8,64,8,128]{3,2,1,0:T(8,128)S(1)}) fusion(f32[1024,8,128]{2,0,1:T(8,128)} %bitcast.240), kind=kLoop, calls=%fused_computation.130 | loop fusion | bytes 8388608
  249.9 52.5 %psum.30 = f32[8]{0:T(128)S(1)} all-reduce(f32[8]{0:T(128)S(1)} %get-tuple-element.149), channel_id=1, replica_groups=mesh['dp'=4,'ctx'=8] {'ctx'}, use_global_device_ids=true, to_apply=%region_11.12 | all-reduce | flops 8 | bytes 64 | tf_op jit(solution)/shard_map/psum | solution.py:154
  302.4 12.4 %psum.31 = f32[8]{0:T(128)} all-reduce(f32[8]{0:T(128)S(1)} %psum.30), channel_id=1, replica_groups=mesh['dp'=4,'ctx'=8] {'dp'}, use_global_device_ids=true, to_apply=%region_12.13 | all-reduce | flops 8 | bytes 64 | tf_op jit(solution)/shard_map/psum | solution.py:154
  318.1 3.8 %gather_fusion = f32[512,1024]{1,0:T(8,128)S(1)} fusion(f32[64,1024]{1,0:T(8,128)} %get-tuple-element.315, s32[1024]{0:T(1024)S(1)} %pad_clamp_fusion), kind=kCustom, calls=%fused_computation | custom fusion | bytes 4196352 | tf_op jit(solution)/shard_map/gather | solution.py:150
  321.9 2.7 gather_fusion.1
  324.6 6.0 %fusion.99 = (bf16[1,512,1024]{2,1,0:T(8,128)(2,1)}, bf16[1,512,1024]{2,1,0:T(8,128)(2,1)}) fusion(f32[512,1024]{1,0:T(8,128)} %gather_fusion.1, f32[512,1024]{1,0:T(8,128)} %collective-permute-done.3, f32[8,64,8,128]{3,2,1,0:T(8,128)} %get-tuple-element.327, pred[512]{0:T(512)(128)(4,1)S(1)} %fusion.108, f32[512,1024]{1,0:T(8,128)S(1)} %gather_fusion, ...), kind=kLoop, calls=%fused_computation.134 | loop fusion | flops 4194304 | bytes 14680576 | tf_op jit(solution)/shard_map/convert_element_type | solution.py:159
  (221 shorter events, 157.6 us)
Async XLA Ops:
  7.2 9.0 %copy-start.3 = (bf16[1,512,1024]{2,1,0:T(8,128)(2,1)S(1)}, bf16[1,512,1024]{2,1,0:T(8,128)(2,1)}, u32[]{:S(2)}) copy-start(bf16[1,512,1024]{2,1,0:T(8,128)(2,1)} %param.18) | copy-start | bytes 3145732
  7.2 31.1 %all-gather.7.cloned.1.call-start = ((), (), s32[]{:S(2)}) async-start(), calls=%async_computation.1 | async-start | bytes 1179648 | tf_op jit(solution)/shard_map/all_gather | solution.py:96
  9.6 54.1 %all-gather.5.cloned.1.call-start = ((), (), s32[]{:S(2)}) async-start(), calls=%async_computation | async-start | bytes 1179648 | tf_op jit(solution)/shard_map/all_gather | solution.py:95
  11.2 306.9 %all-reduce.3.cloned.1.call-start = ((), (), s32[]{:S(2)}) async-start(), calls=%async_computation.2 | async-start | bytes 1048576 | tf_op jit(solution)/shard_map/psum | solution.py:147
  12.8 12.3 %collective-permute-start = (bf16[512,1024]{0,1:T(8,128)(2,1)S(1)}, bf16[512,1024]{0,1:T(8,128)(2,1)}, u32[]{:S(2)}, u32[]{:S(2)}) collective-permute-start(bf16[512,1024]{0,1:T(8,128)(2,1)S(1)} %bitcast.244), channel_id=1, source_target_pairs={{0,1},{1,2},{2,3},{3,4},{4,5},{5,6},{6,7},{8,9},{9,10},{10,11},{11... | collective-permute-start | bytes 3145736 | tf_op jit(solution)/shard_map/ppermute | solution.py:17
  16.7 11.3 %collective-permute-start.1 = (bf16[512,1024]{0,1:T(8,128)(2,1)S(1)}, bf16[512,1024]{0,1:T(8,128)(2,1)}, u32[]{:S(2)}, u32[]{:S(2)}) collective-permute-start(bf16[512,1024]{0,1:T(8,128)(2,1)S(1)} %bitcast.242), channel_id=1, source_target_pairs={{0,1},{1,2},{2,3},{3,4},{4,5},{5,6},{6,7},{8,9},{9,10},{10,11},{11... | collective-permute-start | bytes 3145736 | tf_op jit(solution)/shard_map/ppermute | solution.py:17
  27.9 37.5 %copy-start.2 = (bf16[1,512,1024]{1,2,0:T(8,128)(2,1)S(1)}, bf16[1,512,1024]{1,2,0:T(8,128)(2,1)}, u32[]{:S(2)}) copy-start(bf16[1,512,1024]{1,2,0:T(8,128)(2,1)} %copy.26) | copy-start | bytes 3145732
  28.0 37.5 %copy-start.8 = (f32[8]{0:T(128)S(1)}, f32[8]{0:T(128)}, u32[]{:S(2)}) copy-start(f32[8]{0:T(128)} %param.20) | copy-start | bytes 100
  240.7 3.0 copy-start.1
  242.3 82.3 %collective-permute-start.2 = (f32[512,1024]{1,0:T(8,128)}, f32[512,1024]{1,0:T(8,128)}, u32[]{:S(2)}, u32[]{:S(2)}) collective-permute-start(f32[512,1024]{1,0:T(8,128)} %bitcast.178), channel_id=1, source_target_pairs={{1,0},{2,1},{3,2},{4,3},{5,4},{6,5},{7,6},{9,8},{10,9},{11,10},{12... | collective-permute-start | bytes 6291464 | tf_op jit(solution)/shard_map/ppermute | solution.py:17
  245.4 2.9 copy-start.7
  245.4 3.7 %copy-start.6 = (f32[8,64,128]{2,1,0:T(8,128)S(1)}, f32[8,64,128]{2,1,0:T(8,128)}, u32[]{:S(2)}) copy-start(f32[8,64,128]{2,1,0:T(8,128)} %get-tuple-element.146) | copy-start | bytes 786436
  245.4 69.4 %copy-start.5 = (bf16[8,512,128]{2,1,0:T(8,128)(2,1)S(1)}, bf16[8,512,128]{2,1,0:T(8,128)(2,1)}, u32[]{:S(2)}) copy-start(bf16[8,512,128]{2,1,0:T(8,128)(2,1)} %get-tuple-element.144) | copy-start | bytes 3145732
  247.0 77.5 %collective-permute-start.3 = (f32[512,1024]{1,0:T(8,128)}, f32[512,1024]{1,0:T(8,128)}, u32[]{:S(2)}, u32[]{:S(2)}) collective-permute-start(f32[512,1024]{1,0:T(8,128)} %bitcast.177), channel_id=1, source_target_pairs={{1,0},{2,1},{3,2},{4,3},{5,4},{6,5},{7,6},{9,8},{10,9},{11,10},{12... | collective-permute-start | bytes 6291464 | tf_op jit(solution)/shard_map/ppermute | solution.py:17
  314.8 2.0 copy-start.4
  318.1 3.8 %copy-start = (f32[64,1024]{1,0:T(8,128)S(1)}, f32[64,1024]{1,0:T(8,128)}, u32[]{:S(2)}) copy-start(f32[64,1024]{1,0:T(8,128)} %get-tuple-element.316) | copy-start | bytes 786436
Sparse Core Ops, SparseCore 0:
  9.9 28.2 all-gather.6
  40.1 23.5 all-gather.4
  250.0 59.8 all-reduce.2
